TPU v7x, 512 devices: a whole 4x8x8 slice. The times are simulated.
512 devices in a mesh: bulk: 64 (over x, z, core), span: 8 (over y).
Axes of the slice: x: 4, y: 8, z: 8, core: 2. Of those that a mesh axis runs over, the one named last changes fastest.
Arguments:
- snapshots: float32 [1048576, 128], P(('span', 'bulk'))
- jac_blocks: bfloat16 [8192, 4, 128, 128], P(('span', 'bulk'))
- jac_cols: int32 [8192, 4], P(('span', 'bulk')), may hold values from 0 to 8191, as said below
Outputs:
- modes: float32 [1048576, 128], P(('span', 'bulk'))
- factor: float32 [128, 128], replicated
- jac_modes: bfloat16 [1048576, 128], P(('span', 'bulk'))
- reduced: float32 [128, 128], replicated
Inputs may be any that keep to these rules, and one draw needn't show every extreme that they name: jac_cols[r, 0] = r. Every column block lies in the die region of r (aligned runs of 1024 block rows) and within 16 block rows of the shard of 16 block rows that holds r.
All inputs are finite; a program needn't handle non-finite values.
Results may differ from a plain program's by a relative error of at most 0.0029.
The roundings to bfloat16 on the way count: a program that leaves them out, or rounds other values in their place, can miss the bound.
Values may be sent and summed in bfloat16 or wider, within the bound.
A program may use at most 64 MiB of HBM per device.

v0:
```python
import jax
import jax.numpy as jnp
from jax import lax
from jax.sharding import PartitionSpec as P


def with_halo(array, sides, width):
    for axis, dim in sides:
        size, length = (lax.axis_size(axis), array.shape[dim])
        up = [(i, (i + 1) % size) for i in range(size - 1)]
        down = [(j, i) for i, j in up]
        last = lax.slice_in_dim(array, length - width, length, axis=dim)
        initial = lax.slice_in_dim(array, 0, width, axis=dim)
        before = lax.ppermute(last, axis, up)
        after = lax.ppermute(initial, axis, down)
        array = jnp.concatenate([before, array, after], axis=dim)
    return array


def total_gram(partial_value):
    return lax.psum(partial_value, ("bulk", "span"))


def cholesky_step(data, row_count):
    high = lax.Precision.HIGHEST
    width = data.shape[1]
    partial_value = lax.dot_general(
        data, data, (((0,), (0,)), ((), ())), precision=high, preferred_element_type=jnp.float32
    )
    gram = total_gram(partial_value) / row_count
    lower = jnp.linalg.cholesky(gram)
    inverse = lax.linalg.triangular_solve(
        lower, jnp.eye(width, dtype=jnp.float32), left_side=True, lower=True
    )
    result = jnp.dot(data, inverse.T, precision=high, preferred_element_type=jnp.float32)
    return (result, lower)


def shards(snapshots, jac_blocks, jac_cols):
    high = lax.Precision.HIGHEST
    local_rows, width = snapshots.shape
    block_rows = jac_cols.shape[0]
    blk = jac_blocks.shape[2]
    row_count = local_rows * lax.axis_size(("bulk", "span"))
    first, lower1 = cholesky_step(snapshots, row_count)
    modes, lower2 = cholesky_step(first, row_count)
    factor = jnp.dot(lower2.T, lower1.T, precision=high, preferred_element_type=jnp.float32)
    modes_b = modes.astype(jnp.bfloat16)
    shard_start = (
        lax.axis_index("span") * lax.axis_size("bulk") + lax.axis_index("bulk")
    ) * block_rows
    relative = jac_cols - shard_start
    extended = with_halo(modes_b, (("bulk", 0),), local_rows)
    ext_blocks = extended.reshape(3 * block_rows, blk, width)
    picked = jnp.take(ext_blocks, relative + block_rows, axis=0)
    product = jnp.einsum("rnij,rnjk->rik", jac_blocks, picked, preferred_element_type=jnp.float32)
    jac_modes = product.astype(jnp.bfloat16).reshape(local_rows, width)
    partial_value = lax.dot_general(
        modes,
        jac_modes.astype(jnp.float32),
        (((0,), (0,)), ((), ())),
        precision=high,
        preferred_element_type=jnp.float32,
    )
    reduced = lax.psum(partial_value, ("bulk", "span")) / row_count
    return (modes, factor, jac_modes, reduced)


def solution(mesh):
    return jax.shard_map(
        shards,
        mesh=mesh,
        in_specs=(
            P(("span", "bulk"), None),
            P(("span", "bulk"), None, None, None),
            P(("span", "bulk"), None),
        ),
        out_specs=(P(("span", "bulk"), None), P(), P(("span", "bulk"), None), P()),
        check_vma=False,
    )
```

profile of v0, /device:TPU:1, one launch (start us, length us, event | category | flops | bytes accessed | tf_op | source)
XLA Modules:
  0.0 870.4 jit_solution(4245679873390945482)
XLA Ops:
  7.2 0.0 copy-start
  7.2 0.0 all-reduce.4.cloned.1.call-start
  7.2 4.1 fusion.29
  11.4 0.0 all-reduce.4.cloned.1.call-update
  11.4 0.0 all-reduce.6.cloned.1.call-start
  11.4 266.6 %all-reduce.4.cloned.1.call-done = f32[128,128]{0,1:T(8,128)} async-done(((f32[128,128]{0,1:T(8,128)}), f32[128,128]{0,1:T(8,128)}) %all-reduce.4.cloned.1.call-update) | async-done | bytes 65552 | tf_op jit(solution)/shard_map/psum | solution.py:21
  278.0 0.8 broadcast_multiply_fusion.2
  278.9 0.1 copy.16
  279.0 0.9 fusion.17
  279.8 11.7 %cholesky.44 = f32[128,128]{1,0:T(8,128)S(1)} custom-call(f32[128,128]{1,0:T(8,128)S(1)} %fusion.17), custom_call_target="Cholesky" | custom-call | tf_op jit(solution)/shard_map/jit(cholesky)/cholesky | solution.py:31
  291.6 0.6 compare_reduce_fusion.1
  292.2 0.6 select_bitcast_fusion.1
  292.8 9.8 %custom-call.6 = f32[1,128,128]{1,2,0:T(8,128)S(1)} custom-call(f32[1,128,128]{2,1,0:T(8,128)S(1)} %select_bitcast_fusion.1), custom_call_target="InvertDiagBlocksLowerTriangular" | custom-call | tf_op jit(solution)/shard_map/triangular_solve/custom-call.0 | solution.py:32
  302.6 0.3 fusion.12
  302.9 2.2 fusion.30
  305.1 1.6 fusion.31
  306.8 0.0 copy-start.3
  306.8 0.0 all-reduce.6.cloned.1.call-update
  306.8 0.2 all-reduce.8.cloned.1.call-start
  307.0 250.7 %all-reduce.6.cloned.1.call-done = f32[128,128]{0,1:T(8,128)} async-done(((f32[128,128]{0,1:T(8,128)}), f32[128,128]{0,1:T(8,128)}) %all-reduce.6.cloned.1.call-update) | async-done | bytes 65552 | tf_op jit(solution)/shard_map/psum | solution.py:21
  557.7 0.8 broadcast_multiply_fusion.1
  558.5 0.1 copy.18
  558.6 0.9 fusion.15
  559.5 11.7 %cholesky.55 = f32[128,128]{1,0:T(8,128)S(1)} custom-call(f32[128,128]{1,0:T(8,128)S(1)} %fusion.15), custom_call_target="Cholesky" | custom-call | tf_op jit(solution)/shard_map/jit(cholesky)/cholesky | solution.py:31
  571.2 0.7 compare_reduce_fusion
  572.0 0.7 select_bitcast_fusion
  572.7 9.8 %custom-call.7 = f32[1,128,128]{1,2,0:T(8,128)S(1)} custom-call(f32[1,128,128]{2,1,0:T(8,128)S(1)} %select_bitcast_fusion), custom_call_target="InvertDiagBlocksLowerTriangular" | custom-call | tf_op jit(solution)/shard_map/triangular_solve/custom-call.0 | solution.py:32
  582.5 0.3 fusion.10
  582.8 2.9 fusion.28
  585.7 1.9 collective-permute-start.1
  587.6 3.6 collective-permute-start
  591.3 0.0 copy-done.3
  591.3 0.1 copy.20
  591.4 0.1 reshape.36
  591.5 0.1 copy.19
  591.6 4.8 collective-permute-done.1
  596.4 1.3 collective-permute-done
  597.7 2.3 pad_maximum_fusion
  600.0 3.6 gather_fusion
  603.6 0.0 copy-done
  603.6 0.0 copy-start.1
  603.6 2.5 fusion.6
  606.0 0.0 copy-start.2
  606.0 0.0 copy-done.1
  606.1 1.4 fusion.32
  607.4 0.0 all-reduce.8.cloned.1.call-update
  607.5 2.2 fusion.19
  609.6 252.7 %all-reduce.8.cloned.1.call-done = f32[128,128]{0,1:T(8,128)} async-done(((f32[128,128]{0,1:T(8,128)}), f32[128,128]{0,1:T(8,128)}) %all-reduce.8.cloned.1.call-update) | async-done | bytes 65552 | tf_op jit(solution)/shard_map/psum | solution.py:65
  862.3 0.8 broadcast_multiply_fusion
  863.2 0.7 copy.22
  863.9 0.0 copy-done.2
  (4 shorter events, 0.1 us)
Async XLA Ops:
  7.2 596.4 %copy-start = (bf16[16,4,128,128]{3,2,1,0:T(8,128)(2,1)S(1)}, bf16[16,4,128,128]{3,2,1,0:T(8,128)(2,1)}, u32[]{:S(2)}) copy-start(bf16[16,4,128,128]{3,2,1,0:T(8,128)(2,1)} %param.7) | copy-start | bytes 6291460
  7.2 270.8 %all-reduce.4.cloned.1.call-start = ((), (), s32[]{:S(2)}) async-start(), calls=%async_computation | async-start | bytes 131072 | tf_op jit(solution)/shard_map/psum | solution.py:21
  11.4 546.3 %all-reduce.6.cloned.1.call-start = ((), (), s32[]{:S(2)}) async-start(), calls=%async_computation.1 | async-start | bytes 131072 | tf_op jit(solution)/shard_map/psum | solution.py:21
  306.8 284.5 %copy-start.3 = (s32[16,4]{0,1:T(4,128)S(1)}, s32[16,4]{0,1:T(4,128)}, u32[]{:S(2)}) copy-start(s32[16,4]{0,1:T(4,128)} %param.8) | copy-start | bytes 772
  306.8 555.5 %all-reduce.8.cloned.1.call-start = ((), (), s32[]{:S(2)}) async-start(), calls=%async_computation.2 | async-start | bytes 131072 | tf_op jit(solution)/shard_map/psum | solution.py:65
  585.7 10.7 %collective-permute-start.1 = (bf16[2048,128]{1,0:T(8,128)(2,1)}, bf16[2048,128]{1,0:T(8,128)(2,1)S(1)}, u32[]{:S(2)}, u32[]{:S(2)}) collective-permute-start(bf16[2048,128]{1,0:T(8,128)(2,1)} %get-tuple-element.16), channel_id=1, source_target_pairs={{8,0},{16,8},{24,16},{32,24},{40,32},{48,40},{56,48},{64,56},{72,6... | collective-permute-start | bytes 1572872 | tf_op jit(solution)/shard_map/ppermute | solution.py:15
  587.6 10.1 %collective-permute-start = (bf16[2048,128]{1,0:T(8,128)(2,1)}, bf16[2048,128]{1,0:T(8,128)(2,1)S(1)}, u32[]{:S(2)}, u32[]{:S(2)}) collective-permute-start(bf16[2048,128]{1,0:T(8,128)(2,1)} %get-tuple-element.16), channel_id=1, source_target_pairs={{0,8},{8,16},{16,24},{24,32},{32,40},{40,48},{48,56},{56,64},{64,7... | collective-permute-start | bytes 1572872 | tf_op jit(solution)/shard_map/ppermute | solution.py:14
  603.6 2.5 copy-start.1
  606.0 257.9 %copy-start.2 = (bf16[16,128,128]{1,2,0:T(8,128)(2,1)}, bf16[16,128,128]{1,2,0:T(8,128)(2,1)S(1)}, u32[]{:S(2)}) copy-start(bf16[16,128,128]{1,2,0:T(8,128)(2,1)S(1)} %fusion.6) | copy-start | bytes 1572868
Sparse Core Ops, SparseCore 0:
  13.6 264.4 all-reduce.3
  306.9 250.7 all-reduce.5
  607.6 254.6 all-reduce.7
where the time goes:
time: 871 us; the launch traced here: 870 us
  waiting for transfers between devices  776 us (89%)
  other arithmetic  52.3 us (6%)
  matrix products  17.5 us (2%)
  between operations  13.9 us (2%)
    psum x2, waiting for transfers between devices, total_gram(): return lax.psum(partial_value, ('bulk', 'span'))  517 us
    psum x1, waiting for transfers between devices, shards(): reduced = lax.psum(partial_value, ('bulk', 'span')) / row_count  253 us
    another operation x6, other arithmetic, cholesky_step(): lower = jnp.linalg.cholesky(gram)  24.9 us
    another operation x4, other arithmetic, cholesky_step(): lax.linalg.triangular_solve(lower, jnp.eye(width, dtype=jnp.float32), lef...  20.9 us
  transfers between devices with their start and end apart: 5, of which 5 were waited for; matrix products, arithmetic and copies ran while one was open for 0% of the time, Pallas kernels for 0%

commit v1 on v0

--- a/solution.py
+++ b/solution.py
@@ -2,6 +2,12 @@
 import jax.numpy as jnp
 from jax import lax
 from jax.sharding import PartitionSpec as P
+
+
+def add_all(x, axis):
+    shards = lax.all_gather(x, axis, axis=0, tiled=False)
+    summed = shards.sum(axis=0)
+    return summed
 
 
 def with_halo(array, sides, width):
@@ -62,7 +68,7 @@
         precision=high,
         preferred_element_type=jnp.float32,
     )
-    reduced = lax.psum(partial_value, ("bulk", "span")) / row_count
+    reduced = add_all(partial_value, ("bulk", "span")) / row_count
     return (modes, factor, jac_modes, reduced)
 
 

time: 871 us -> 786 us (0.902)
  waiting for transfers between devices: 776 us -> 678 us
  other arithmetic: 52.3 us -> 64.6 us
    psum x1 -> x0, waiting for transfers between devices: 253 us -> none  [shards(): reduced = lax.psum(partial_value, ('bulk', 'span')) / row_count]
    all_gather x0 -> x1, waiting for transfers between devices: none -> 155 us  [add_all(): shards = lax.all_gather(x, axis, axis=0, tiled=False)]
    reduce_sum x0 -> x1, other arithmetic: none -> 13.1 us  [add_all(): summed = shards.sum(axis=0)]
where the time goes in v1:
time: 786 us; the launch traced here: 785 us
  waiting for transfers between devices  678 us (86%)
  other arithmetic  64.6 us (8%)
  matrix products  17.8 us (2%)
  between operations  13.9 us (2%)
    psum x2, waiting for transfers between devices, total_gram(): return lax.psum(partial_value, ('bulk', 'span'))  517 us
    all_gather x1, waiting for transfers between devices, add_all(): shards = lax.all_gather(x, axis, axis=0, tiled=False)  155 us
    another operation x6, other arithmetic, cholesky_step(): lower = jnp.linalg.cholesky(gram)  24.9 us
    another operation x4, other arithmetic, cholesky_step(): lax.linalg.triangular_solve(lower, jnp.eye(width, dtype=jnp.float32), lef...  20.9 us
  transfers between devices with their start and end apart: 5, of which 5 were waited for; matrix products, arithmetic and copies ran while one was open for 0% of the time, Pallas kernels for 0%

profile of v1, /device:TPU:1, one launch (start us, length us, event | category | flops | bytes accessed | tf_op | source)
XLA Modules:
  0.0 785.4 jit_solution(4662453676478478288)
XLA Ops:
  7.2 0.0 copy-start
  7.2 0.0 all-reduce.3.cloned.1.call-start
  7.2 4.1 fusion.29
  11.4 0.0 all-reduce.3.cloned.1.call-update
  11.4 0.0 all-reduce.5.cloned.1.call-start
  11.4 266.6 %all-reduce.3.cloned.1.call-done = f32[128,128]{0,1:T(8,128)} async-done(((f32[128,128]{0,1:T(8,128)}), f32[128,128]{0,1:T(8,128)}) %all-reduce.3.cloned.1.call-update) | async-done | bytes 65552 | tf_op jit(solution)/shard_map/psum | solution.py:27
  278.0 0.8 broadcast_multiply_fusion.2
  278.9 0.1 copy.22
  279.0 0.9 fusion.17
  279.8 11.7 %cholesky.44 = f32[128,128]{1,0:T(8,128)S(1)} custom-call(f32[128,128]{1,0:T(8,128)S(1)} %fusion.17), custom_call_target="Cholesky" | custom-call | tf_op jit(solution)/shard_map/jit(cholesky)/cholesky | solution.py:37
  291.6 0.7 compare_reduce_fusion.1
  292.3 0.7 select_bitcast_fusion.1
  293.0 9.8 %custom-call.6 = f32[1,128,128]{1,2,0:T(8,128)S(1)} custom-call(f32[1,128,128]{2,1,0:T(8,128)S(1)} %select_bitcast_fusion.1), custom_call_target="InvertDiagBlocksLowerTriangular" | custom-call | tf_op jit(solution)/shard_map/triangular_solve/custom-call.0 | solution.py:38
  302.8 0.3 fusion.12
  303.1 2.2 fusion.30
  305.3 1.6 fusion.31
  306.9 0.0 copy-start.3
  306.9 0.0 all-reduce.5.cloned.1.call-update
  307.0 0.2 all-gather.3.cloned.1.call-start
  307.2 250.7 %all-reduce.5.cloned.1.call-done = f32[128,128]{0,1:T(8,128)} async-done(((f32[128,128]{0,1:T(8,128)}), f32[128,128]{0,1:T(8,128)}) %all-reduce.5.cloned.1.call-update) | async-done | bytes 65552 | tf_op jit(solution)/shard_map/psum | solution.py:27
  557.9 0.8 broadcast_multiply_fusion.1
  558.8 0.1 copy.24
  558.9 0.9 fusion.15
  559.7 11.7 %cholesky.55 = f32[128,128]{1,0:T(8,128)S(1)} custom-call(f32[128,128]{1,0:T(8,128)S(1)} %fusion.15), custom_call_target="Cholesky" | custom-call | tf_op jit(solution)/shard_map/jit(cholesky)/cholesky | solution.py:37
  571.5 0.7 compare_reduce_fusion
  572.1 0.6 select_bitcast_fusion
  572.8 9.8 %custom-call.7 = f32[1,128,128]{1,2,0:T(8,128)S(1)} custom-call(f32[1,128,128]{2,1,0:T(8,128)S(1)} %select_bitcast_fusion), custom_call_target="InvertDiagBlocksLowerTriangular" | custom-call | tf_op jit(solution)/shard_map/triangular_solve/custom-call.0 | solution.py:38
  582.6 0.3 fusion.10
  582.9 2.9 fusion.28
  585.8 1.9 collective-permute-start.1
  587.7 3.6 collective-permute-start
  591.4 0.0 copy-done.3
  591.4 0.1 copy.25
  591.5 0.1 copy.26
  591.6 0.1 reshape.36
  591.7 4.8 collective-permute-done.1
  596.5 1.3 collective-permute-done
  597.8 2.3 pad_maximum_fusion
  600.1 3.6 gather_fusion
  603.7 0.0 copy-done
  603.7 0.0 copy-start.1
  603.7 2.5 fusion.6
  606.2 0.0 copy-start.2
  606.2 0.0 copy-done.1
  606.2 1.7 fusion.32
  607.9 0.0 all-gather.3.cloned.1.call-update
  607.9 2.2 fusion.19
  610.1 154.9 %all-gather.3.cloned.1.call-done = f32[65536,128]{1,0:T(8,128)} async-done(((f32[128,128]{1,0:T(8,128)}), f32[65536,128]{1,0:T(8,128)}) %all-gather.3.cloned.1.call-update) | async-done | bytes 33554448 | tf_op jit(solution)/shard_map/all_gather | solution.py:8
  764.9 13.1 %reduce_sum.9 = f32[128,128]{1,0:T(8,128)S(1)} reduce(f32[512,128,128]{2,1,0:T(8,128)} %bitcast.40, f32[]{:T(128)} %constant.65.clone.1), dimensions={0}, to_apply=%region_4.7 | reduce | flops 8372224 | bytes 33619972 | tf_op jit(solution)/shard_map/reduce_sum | solution.py:9
  778.0 0.0 copy-done.2
  778.0 0.1 copy.27
  778.1 0.7 copy.28
  (5 shorter events, 0.1 us)
Async XLA Ops:
  7.2 596.5 %copy-start = (bf16[16,4,128,128]{3,2,1,0:T(8,128)(2,1)S(1)}, bf16[16,4,128,128]{3,2,1,0:T(8,128)(2,1)}, u32[]{:S(2)}) copy-start(bf16[16,4,128,128]{3,2,1,0:T(8,128)(2,1)} %param.7) | copy-start | bytes 6291460
  7.2 270.8 %all-reduce.3.cloned.1.call-start = ((), (), s32[]{:S(2)}) async-start(), calls=%async_computation | async-start | bytes 131072 | tf_op jit(solution)/shard_map/psum | solution.py:27
  11.4 546.5 %all-reduce.5.cloned.1.call-start = ((), (), s32[]{:S(2)}) async-start(), calls=%async_computation.1 | async-start | bytes 131072 | tf_op jit(solution)/shard_map/psum | solution.py:27
  306.9 284.5 %copy-start.3 = (s32[16,4]{0,1:T(4,128)S(1)}, s32[16,4]{0,1:T(4,128)}, u32[]{:S(2)}) copy-start(s32[16,4]{0,1:T(4,128)} %param.8) | copy-start | bytes 772
  307.0 458.0 %all-gather.3.cloned.1.call-start = ((), (), s32[]{:S(2)}) async-start(), calls=%async_computation.2 | async-start | bytes 33619968 | tf_op jit(solution)/shard_map/all_gather | solution.py:8
  585.8 10.7 %collective-permute-start.1 = (bf16[2048,128]{1,0:T(8,128)(2,1)}, bf16[2048,128]{1,0:T(8,128)(2,1)S(1)}, u32[]{:S(2)}, u32[]{:S(2)}) collective-permute-start(bf16[2048,128]{1,0:T(8,128)(2,1)} %get-tuple-element.20), channel_id=1, source_target_pairs={{8,0},{16,8},{24,16},{32,24},{40,32},{48,40},{56,48},{64,56},{72,6... | collective-permute-start | bytes 1572872 | tf_op jit(solution)/shard_map/ppermute | solution.py:21
  587.7 10.1 %collective-permute-start = (bf16[2048,128]{1,0:T(8,128)(2,1)}, bf16[2048,128]{1,0:T(8,128)(2,1)S(1)}, u32[]{:S(2)}, u32[]{:S(2)}) collective-permute-start(bf16[2048,128]{1,0:T(8,128)(2,1)} %get-tuple-element.20), channel_id=1, source_target_pairs={{0,8},{8,16},{16,24},{24,32},{32,40},{40,48},{48,56},{56,64},{64,7... | collective-permute-start | bytes 1572872 | tf_op jit(solution)/shard_map/ppermute | solution.py:20
  603.7 2.5 copy-start.1
  606.2 171.9 %copy-start.2 = (bf16[16,128,128]{1,2,0:T(8,128)(2,1)}, bf16[16,128,128]{1,2,0:T(8,128)(2,1)S(1)}, u32[]{:S(2)}) copy-start(bf16[16,128,128]{1,2,0:T(8,128)(2,1)S(1)} %fusion.6) | copy-start | bytes 1572868
Sparse Core Ops, SparseCore 0:
  13.6 264.4 all-reduce.2
  307.1 250.7 all-reduce.4
  608.0 156.8 all-gather.2

commit v2 on v0

--- a/solution.py
+++ b/solution.py
@@ -62,7 +62,7 @@
         precision=high,
         preferred_element_type=jnp.float32,
     )
-    reduced = lax.psum(partial_value, ("bulk", "span")) / row_count
+    reduced = lax.psum(lax.psum(partial_value, "bulk"), axis_name="span") / row_count
     return (modes, factor, jac_modes, reduced)
 
 

time: 871 us -> 865 us (level)
  waiting for transfers between devices: 776 us -> 767 us
    psum x1 -> x2, waiting for transfers between devices: 253 us -> 243 us  [the longest x1 175 us: shards(): lax.psum(partial_value, 'bulk')]
  transfers between devices with their start and end apart: 5 -> 6, of which waited for: 5 -> 6; matrix products, arithmetic and copies ran while one was open for 0% -> 0% of each run, Pallas kernels for 0% -> 0%
where the time goes in v2:
time: 865 us; the launch traced here: 861 us
  waiting for transfers between devices  767 us (89%)
  other arithmetic  52.3 us (6%)
  matrix products  17.5 us (2%)
  between operations  13.9 us (2%)
    psum x2, waiting for transfers between devices, total_gram(): return lax.psum(partial_value, ('bulk', 'span'))  517 us
    psum x1, waiting for transfers between devices, shards(): lax.psum(partial_value, 'bulk')  175 us
    psum x1, waiting for transfers between devices, shards(): lax.psum(lax.psum(partial_value, 'bulk'), axis_name='span') / row_count  67.9 us
    another operation x6, other arithmetic, cholesky_step(): lower = jnp.linalg.cholesky(gram)  24.9 us
    another operation x4, other arithmetic, cholesky_step(): lax.linalg.triangular_solve(lower, jnp.eye(width, dtype=jnp.float32), lef...  20.9 us
  transfers between devices with their start and end apart: 6, of which 6 were waited for; matrix products, arithmetic and copies ran while one was open for 0% of the time, Pallas kernels for 0%

profile of v2, /device:TPU:1, one launch (start us, length us, event | category | flops | bytes accessed | tf_op | source)
XLA Modules:
  0.0 861.0 jit_solution(17949244246582807750)
XLA Ops:
  7.2 0.0 copy-start
  7.2 0.0 all-reduce.5.cloned.1.call-start
  7.2 4.1 fusion.29
  11.4 0.0 all-reduce.5.cloned.1.call-update
  11.4 0.0 all-reduce.7.cloned.1.call-start
  11.4 266.6 %all-reduce.5.cloned.1.call-done = f32[128,128]{0,1:T(8,128)} async-done(((f32[128,128]{0,1:T(8,128)}), f32[128,128]{0,1:T(8,128)}) %all-reduce.5.cloned.1.call-update) | async-done | bytes 65552 | tf_op jit(solution)/shard_map/psum | solution.py:21
  278.0 0.8 broadcast_multiply_fusion.2
  278.9 0.1 copy.16
  279.0 0.9 fusion.17
  279.8 11.7 %cholesky.44 = f32[128,128]{1,0:T(8,128)S(1)} custom-call(f32[128,128]{1,0:T(8,128)S(1)} %fusion.17), custom_call_target="Cholesky" | custom-call | tf_op jit(solution)/shard_map/jit(cholesky)/cholesky | solution.py:31
  291.6 0.6 compare_reduce_fusion.1
  292.2 0.6 select_bitcast_fusion.1
  292.8 9.8 %custom-call.6 = f32[1,128,128]{1,2,0:T(8,128)S(1)} custom-call(f32[1,128,128]{2,1,0:T(8,128)S(1)} %select_bitcast_fusion.1), custom_call_target="InvertDiagBlocksLowerTriangular" | custom-call | tf_op jit(solution)/shard_map/triangular_solve/custom-call.0 | solution.py:32
  302.6 0.3 fusion.12
  302.9 2.2 fusion.30
  305.1 1.6 fusion.31
  306.8 0.0 copy-start.3
  306.8 0.0 all-reduce.7.cloned.1.call-update
  306.8 0.2 all-reduce.9.cloned.1.call-start
  307.0 250.7 %all-reduce.7.cloned.1.call-done = f32[128,128]{0,1:T(8,128)} async-done(((f32[128,128]{0,1:T(8,128)}), f32[128,128]{0,1:T(8,128)}) %all-reduce.7.cloned.1.call-update) | async-done | bytes 65552 | tf_op jit(solution)/shard_map/psum | solution.py:21
  557.7 0.8 broadcast_multiply_fusion.1
  558.5 0.1 copy.18
  558.6 0.9 fusion.15
  559.5 11.7 %cholesky.55 = f32[128,128]{1,0:T(8,128)S(1)} custom-call(f32[128,128]{1,0:T(8,128)S(1)} %fusion.15), custom_call_target="Cholesky" | custom-call | tf_op jit(solution)/shard_map/jit(cholesky)/cholesky | solution.py:31
  571.2 0.7 compare_reduce_fusion
  572.0 0.7 select_bitcast_fusion
  572.7 9.8 %custom-call.7 = f32[1,128,128]{1,2,0:T(8,128)S(1)} custom-call(f32[1,128,128]{2,1,0:T(8,128)S(1)} %select_bitcast_fusion), custom_call_target="InvertDiagBlocksLowerTriangular" | custom-call | tf_op jit(solution)/shard_map/triangular_solve/custom-call.0 | solution.py:32
  582.5 0.3 fusion.10
  582.8 2.9 fusion.28
  585.7 1.9 collective-permute-start.1
  587.6 3.6 collective-permute-start
  591.3 0.0 copy-done.3
  591.3 0.1 copy.20
  591.4 0.1 reshape.36
  591.5 0.1 copy.19
  591.6 4.8 collective-permute-done.1
  596.4 1.3 collective-permute-done
  597.7 2.3 pad_maximum_fusion
  600.0 3.6 gather_fusion
  603.6 0.0 copy-done
  603.6 0.0 copy-start.1
  603.6 2.5 fusion.6
  606.0 0.0 copy-start.2
  606.0 0.0 copy-done.1
  606.1 1.4 fusion.32
  607.4 0.0 all-reduce.9.cloned.1.call-update
  607.5 0.0 all-reduce.11.cloned.1.call-start
  607.5 175.3 %all-reduce.9.cloned.1.call-done = f32[128,128]{0,1:T(8,128)} async-done(((f32[128,128]{0,1:T(8,128)}), f32[128,128]{0,1:T(8,128)}) %all-reduce.9.cloned.1.call-update) | async-done | bytes 65552 | tf_op jit(solution)/shard_map/psum | solution.py:65
  782.8 0.0 all-reduce.11.cloned.1.call-update
  782.8 2.2 fusion.19
  785.0 67.9 %all-reduce.11.cloned.1.call-done = f32[128,128]{0,1:T(8,128)} async-done(((f32[128,128]{0,1:T(8,128)}), f32[128,128]{0,1:T(8,128)}) %all-reduce.11.cloned.1.call-update) | async-done | bytes 65552 | tf_op jit(solution)/shard_map/psum | solution.py:65
  852.9 0.8 broadcast_multiply_fusion
  853.7 0.7 copy.22
  854.5 0.0 copy-done.2
  (4 shorter events, 0.1 us)
Async XLA Ops:
  7.2 596.4 %copy-start = (bf16[16,4,128,128]{3,2,1,0:T(8,128)(2,1)S(1)}, bf16[16,4,128,128]{3,2,1,0:T(8,128)(2,1)}, u32[]{:S(2)}) copy-start(bf16[16,4,128,128]{3,2,1,0:T(8,128)(2,1)} %param.7) | copy-start | bytes 6291460
  7.2 270.8 %all-reduce.5.cloned.1.call-start = ((), (), s32[]{:S(2)}) async-start(), calls=%async_computation | async-start | bytes 131072 | tf_op jit(solution)/shard_map/psum | solution.py:21
  11.4 546.3 %all-reduce.7.cloned.1.call-start = ((), (), s32[]{:S(2)}) async-start(), calls=%async_computation.1 | async-start | bytes 131072 | tf_op jit(solution)/shard_map/psum | solution.py:21
  306.8 284.5 %copy-start.3 = (s32[16,4]{0,1:T(4,128)S(1)}, s32[16,4]{0,1:T(4,128)}, u32[]{:S(2)}) copy-start(s32[16,4]{0,1:T(4,128)} %param.8) | copy-start | bytes 772
  306.8 476.0 %all-reduce.9.cloned.1.call-start = ((), (), s32[]{:S(2)}) async-start(), calls=%async_computation.2 | async-start | bytes 131072 | tf_op jit(solution)/shard_map/psum | solution.py:65
  585.7 10.7 %collective-permute-start.1 = (bf16[2048,128]{1,0:T(8,128)(2,1)}, bf16[2048,128]{1,0:T(8,128)(2,1)S(1)}, u32[]{:S(2)}, u32[]{:S(2)}) collective-permute-start(bf16[2048,128]{1,0:T(8,128)(2,1)} %get-tuple-element.16), channel_id=1, source_target_pairs={{8,0},{16,8},{24,16},{32,24},{40,32},{48,40},{56,48},{64,56},{72,6... | collective-permute-start | bytes 1572872 | tf_op jit(solution)/shard_map/ppermute | solution.py:15
  587.6 10.1 %collective-permute-start = (bf16[2048,128]{1,0:T(8,128)(2,1)}, bf16[2048,128]{1,0:T(8,128)(2,1)S(1)}, u32[]{:S(2)}, u32[]{:S(2)}) collective-permute-start(bf16[2048,128]{1,0:T(8,128)(2,1)} %get-tuple-element.16), channel_id=1, source_target_pairs={{0,8},{8,16},{16,24},{24,32},{32,40},{40,48},{48,56},{56,64},{64,7... | collective-permute-start | bytes 1572872 | tf_op jit(solution)/shard_map/ppermute | solution.py:14
  603.6 2.5 copy-start.1
  606.0 248.4 %copy-start.2 = (bf16[16,128,128]{1,2,0:T(8,128)(2,1)}, bf16[16,128,128]{1,2,0:T(8,128)(2,1)S(1)}, u32[]{:S(2)}) copy-start(bf16[16,128,128]{1,2,0:T(8,128)(2,1)S(1)} %fusion.6) | copy-start | bytes 1572868
  607.5 245.4 %all-reduce.11.cloned.1.call-start = ((), (), s32[]{:S(2)}) async-start(), calls=%async_computation.3 | async-start | bytes 131072 | tf_op jit(solution)/shard_map/psum | solution.py:65
Sparse Core Ops, SparseCore 0:
  13.6 264.4 all-reduce.4
  306.9 250.7 all-reduce.6
  607.6 175.1 all-reduce.8
  785.0 67.8 all-reduce.10
